TPU v7x, 256 devices: a whole 4x4x8 slice. The times are simulated.
256 devices in a mesh: frame: 32 (over z_lo, y, core), mod: 2 (over z_hi), row: 4 (over x).
Axes of the slice: x: 4, y: 4, z: 8 (z_hi: 2, z_lo: 4; z = z_hi * 4 + z_lo), core: 2. Of those that a mesh axis runs over, the one named last changes fastest.
Arguments:
- amplitude: float32 [512, 512], P('row'), may hold values from 0.25 to 1.75
- pupil_mask: int32 [512, 512], P('row'), may hold values 0 or 1
- phase_common: float32 [512, 512], P('row'), may hold values from -3 to 3
- screens: float32 [32, 512, 512], P('frame', 'row'), may hold values from -6 to 6
- offsets: int32 [2, 2], P('mod'), may hold values from -8 to 8
- measured: float32 [32, 1024, 1024], P('frame', 'row'), may hold values from 0 to 0.5
- valid: int32 [1024, 1024], P('row'), may hold values 0 or 1
Outputs:
- intensity: float32 [32, 1024, 1024], P('frame', 'row', 'mod')
- phase_grad: float32 [512, 512], P('row')
- amp_grad: float32 [512, 512], P('row')
All inputs are finite; a program needn't handle non-finite values. No bound on the sum of `pupil_mask` or of `valid` on one device may be relied on, other than what follows from the above.
Results may differ from a plain program's by a relative error of at most 0.017.
Values may be sent and summed in bfloat16 or wider, within the bound.
No kernel may reach another device: no remote copies, remote signals or barrier semaphores. Data moves between devices by JAX's collectives and lax.ppermute only.
A program may use at most 64 MiB of HBM per device.

v0:
```python
import math

import jax
import jax.numpy as jnp
from jax import lax
from jax.sharding import PartitionSpec as P


def twiddle(row_index, col_index, period, direction):
    product = row_index[:, None] * col_index[None, :] % period
    angles = direction * 2.0 * math.pi / period * product.astype(jnp.float32)
    return (jnp.cos(angles), jnp.sin(angles))


def pyramid(row_index, col_index, offset_pair, pupil_width, full_width):
    spread = (
        jnp.abs(row_index - offset_pair[0])[:, None] + jnp.abs(col_index - offset_pair[1])[None, :]
    )
    angles = math.pi / full_width * (pupil_width * spread % (2 * full_width)).astype(jnp.float32)
    return (jnp.cos(angles), jnp.sin(angles))


def to_bfloat(complex_pair):
    return (complex_pair[0].astype(jnp.bfloat16), complex_pair[1].astype(jnp.bfloat16))


def right_blocks(table_pair, conjugated):
    real_part, imag_part = table_pair
    if conjugated:
        imag_part = -imag_part
    return (
        jnp.concatenate([real_part, imag_part], axis=1),
        jnp.concatenate([-imag_part, real_part], axis=1),
    )


def left_blocks(table_pair, conjugated):
    real_part, imag_part = table_pair
    if conjugated:
        imag_part = -imag_part
    return (
        jnp.concatenate([real_part, imag_part], axis=0),
        jnp.concatenate([-imag_part, real_part], axis=0),
    )


def right_product(field_pair, blocks):
    half_cols = blocks[0].shape[1] // 2
    product = jnp.dot(field_pair[0], blocks[0], preferred_element_type=jnp.float32) + jnp.dot(
        field_pair[1], blocks[1], preferred_element_type=jnp.float32
    )
    return (product[:, :half_cols], product[:, half_cols:])


def left_product(blocks, field_pair):
    height = blocks[0].shape[0] // 2
    product = jnp.dot(blocks[0], field_pair[0], preferred_element_type=jnp.float32) + jnp.dot(
        blocks[1], field_pair[1], preferred_element_type=jnp.float32
    )
    return (product[:height], product[height:])


def modulate(focal_field, face_mask):
    return to_bfloat(
        (
            focal_field[0] * face_mask[0] - focal_field[1] * face_mask[1],
            focal_field[0] * face_mask[1] + focal_field[1] * face_mask[0],
        )
    )


def demodulate_add(running_pair, back_pass, face_mask):
    return (
        running_pair[0] + face_mask[0] * back_pass[0] + face_mask[1] * back_pass[1],
        running_pair[1] + face_mask[0] * back_pass[1] - face_mask[1] * back_pass[0],
    )


def shards(amplitude, pupil_mask, phase_common, screens, offsets, measured, valid):
    rows_count = lax.axis_size("row")
    mods_count = lax.axis_size("mod")
    row_at = lax.axis_index("row")
    mod_at = lax.axis_index("mod")
    pupil_rows, pupil_width = amplitude.shape
    det_rows, full_width = valid.shape
    columns = full_width // rows_count
    share_width = full_width // mods_count
    mod_total = offsets.shape[0] * mods_count
    frame_total = screens.shape[0] * lax.axis_size("frame")
    pupil_idx = jnp.arange(pupil_width, dtype=jnp.int32) - pupil_width // 2
    focal_idx = jnp.arange(full_width, dtype=jnp.int32) - full_width // 2
    own_columns = lax.dynamic_slice_in_dim(focal_idx, row_at * columns, columns)
    w_tab = to_bfloat(twiddle(pupil_idx, focal_idx, full_width, -1.0))
    wt_tab = to_bfloat(twiddle(focal_idx, pupil_idx, full_width, -1.0))
    g_raw = twiddle(focal_idx, focal_idx, full_width, 1.0)
    g_tab = to_bfloat((g_raw[0] / full_width, g_raw[1] / full_width))
    w_right = right_blocks(w_tab, False)
    wt_left = left_blocks(wt_tab, False)
    g_right = right_blocks(g_tab, False)
    g_right_conj = right_blocks(g_tab, True)
    w_left_conj = left_blocks(w_tab, True)
    wt_right_conj = right_blocks(wt_tab, True)
    mask_float = pupil_mask.astype(jnp.float32)
    weight = amplitude * mask_float
    live_pixels = valid.astype(jnp.float32)
    adjoint_scale = 2.0 / mod_total
    phase_total = phase_common + screens[0]
    cosine = jnp.cos(phase_total)
    sine_part = jnp.sin(phase_total)
    pupil_field = (weight * cosine, weight * sine_part)
    first_pass = to_bfloat(right_product(to_bfloat(pupil_field), w_right))
    first_pass = (
        lax.all_to_all(first_pass[0], "row", split_axis=1, concat_axis=0, tiled=True),
        lax.all_to_all(first_pass[1], "row", split_axis=1, concat_axis=0, tiled=True),
    )
    focal_field = to_bfloat(left_product(wt_left, first_pass))
    g_left = left_blocks(g_tab, False)

    def forward(running, offset_pair):
        face_mask = pyramid(focal_idx, own_columns, offset_pair, pupil_width, full_width)
        inner_pass = to_bfloat(left_product(g_left, modulate(focal_field, face_mask)))
        inner_pass = (
            lax.all_to_all(inner_pass[0], "row", split_axis=0, concat_axis=1, tiled=True),
            lax.all_to_all(inner_pass[1], "row", split_axis=0, concat_axis=1, tiled=True),
        )
        detector = right_product(inner_pass, g_right)
        return (running + detector[0] * detector[0] + detector[1] * detector[1], detector)

    running, detectors = lax.scan(forward, jnp.zeros((det_rows, full_width), jnp.float32), offsets)
    target = measured[0]
    total_sum = lax.psum(running.astype(jnp.bfloat16), "mod").astype(jnp.float32)
    intensity_full = total_sum / mod_total
    residual = live_pixels * (intensity_full - target)
    image_part = lax.dynamic_slice_in_dim(intensity_full, mod_at * share_width, share_width, 1)
    images = [image_part]
    g_left_conj = left_blocks(g_tab, True)

    def adjoint(running_pair, scan_parts):
        offset_pair, det_real, det_imag = scan_parts
        face_mask = pyramid(focal_idx, own_columns, offset_pair, pupil_width, full_width)
        weighted = to_bfloat(
            (adjoint_scale * residual * det_real, adjoint_scale * residual * det_imag)
        )
        inner_pass = to_bfloat(right_product(weighted, g_right_conj))
        inner_pass = (
            lax.all_to_all(inner_pass[0], "row", split_axis=1, concat_axis=0, tiled=True),
            lax.all_to_all(inner_pass[1], "row", split_axis=1, concat_axis=0, tiled=True),
        )
        back_pass = left_product(g_left_conj, inner_pass)
        return (demodulate_add(running_pair, back_pass, face_mask), None)

    zero_focal = jnp.zeros((full_width, columns), jnp.float32)
    group_sum, _ = lax.scan(
        adjoint, (zero_focal, zero_focal), (offsets, detectors[0], detectors[1])
    )
    spread_back = to_bfloat(left_product(w_left_conj, to_bfloat(group_sum)))
    spread_back = (
        lax.all_to_all(spread_back[0], "row", split_axis=0, concat_axis=1, tiled=True),
        lax.all_to_all(spread_back[1], "row", split_axis=0, concat_axis=1, tiled=True),
    )
    pupil_back = right_product(spread_back, wt_right_conj)
    phase_sum = pupil_back[1] * pupil_field[0] - pupil_back[0] * pupil_field[1]
    amp_sum = mask_float * (pupil_back[0] * cosine + pupil_back[1] * sine_part)
    gradients = lax.psum((phase_sum / frame_total, amp_sum / frame_total), ("frame", "mod"))
    return (jnp.stack(images, axis=0), gradients[0], gradients[1])


def solution(mesh):
    placed = (
        P("row", None),
        P("row", None),
        P("row", None),
        P("frame", "row", None),
        P("mod", None),
        P("frame", "row", None),
        P("row", None),
    )
    return jax.shard_map(
        shards,
        mesh=mesh,
        in_specs=placed,
        out_specs=(P("frame", "row", "mod"), P("row", None), P("row", None)),
        check_vma=False,
    )
```

profile of v0, /device:TPU:2, one launch (start us, length us, event | category | flops | bytes accessed | tf_op | source)
XLA Modules:
  0.0 469.3 jit_solution(10787694055746772982)
XLA Ops:
  7.2 9.0 %cosine_convert_fusion = (bf16[512,1024]{1,0:T(8,128)(2,1)S(1)}, bf16[512,1024]{1,0:T(8,128)(2,1)S(1)}) fusion(s32[1024]{0:T(1024)S(1)} %iota_add_fusion, s32[512]{0:T(512)S(1)} %iota_add_fusion.1), kind=kLoop, calls=%fused_computation.91 | loop fusion | flops 8388608 | bytes 2103296 | tf_op jit(solution)/shard_map/convert_element_type | solution.py:24
  16.2 8.4 %fusion.98 = bf16[512,1024]{1,0:T(8,128)(2,1)S(1)} fusion(s32[1024]{0:T(1024)S(1)} %iota_add_fusion, s32[512]{0:T(512)S(1)} %iota_add_fusion.1), kind=kLoop, calls=%fused_computation.136 | loop fusion | flops 9437184 | bytes 1054720 | tf_op jit(solution)/shard_map/neg | solution.py:33
  28.2 6.3 %all-to-all-start = ((bf16[128,4,256]{2,0,1:T(8,128)(2,1)}), bf16[128,4,256]{2,0,1:T(8,128)(2,1)}, u32[]{:S(2)}, u32[]{:S(2)}) async-start(bf16[128,4,256]{2,0,1:T(8,128)(2,1)} %bitcast.79), calls=%async_computation | async-start | bytes 524288 | tf_op jit(solution)/shard_map/all_to_all | solution.py:113
  34.4 9.7 %cosine_convert_fusion.1 = (bf16[1024,512]{1,0:T(8,128)(2,1)S(1)}, bf16[1024,512]{1,0:T(8,128)(2,1)}) fusion(s32[512]{0:T(512)S(1)} %iota_add_fusion.1, s32[1024]{0:T(1024)S(1)} %iota_add_fusion), kind=kLoop, calls=%fused_computation.93 | loop fusion | flops 8388608 | bytes 2103296 | tf_op jit(solution)/shard_map/convert_element_type | solution.py:24
  44.2 9.2 %fusion.97 = bf16[1024,512]{1,0:T(8,128)(2,1)} fusion(s32[512]{0:T(512)S(1)} %iota_add_fusion.1, s32[1024]{0:T(1024)S(1)} %iota_add_fusion), kind=kLoop, calls=%fused_computation.135 | loop fusion | flops 9437184 | bytes 1054720 | tf_op jit(solution)/shard_map/neg | solution.py:43
  53.4 18.9 %multiply_convert_fusion = (bf16[1024,1024]{1,0:T(8,128)(2,1)}, bf16[1024,1024]{1,0:T(8,128)(2,1)S(1)}) fusion(s32[1024]{0:T(1024)S(1)} %iota_add_fusion), kind=kLoop, calls=%fused_computation.32 | loop fusion | flops 18874368 | bytes 4198400 | tf_op jit(solution)/shard_map/convert_element_type | solution.py:24
  72.3 17.7 %fusion.82 = bf16[1024,1024]{1,0:T(8,128)(2,1)} fusion(s32[1024]{0:T(1024)S(1)} %iota_add_fusion), kind=kLoop, calls=%fused_computation.121 | loop fusion | flops 19922944 | bytes 2101248 | tf_op jit(solution)/shard_map/neg | solution.py:43
  92.6 5.0 %all-to-all-start.1 = ((bf16[128,4,256]{2,0,1:T(8,128)(2,1)}), bf16[128,4,256]{2,0,1:T(8,128)(2,1)}, u32[]{:S(2)}, u32[]{:S(2)}) async-start(bf16[128,4,256]{2,0,1:T(8,128)(2,1)} %bitcast.84), calls=%async_computation.1 | async-start | bytes 524288 | tf_op jit(solution)/shard_map/all_to_all | solution.py:114
  105.6 5.4 %fusion.4 = f32[2048,256]{1,0:T(8,128)S(1)} fusion(bf16[1024,1024]{1,0:T(8,128)(2,1)S(1)} %get-tuple-element.87, bf16[1024,1024]{1,0:T(8,128)(2,1)S(1)} %copy-done.3, s32[256]{0:T(256)S(1)} %subtract_abs_fusion.1, s32[1024]{0:T(1024)S(1)} %subtract_abs_fusion, bf16[2048,256]{1,0:T(8,128)(2,1)S(1)} %fusion.23), kind=kOutput, calls=%fused_computation.17 | convolution fusion | flops 1087635456 | bytes 7345152 | tf_op jit(solution)/shard_map/while/body/eval_jaxpr/dot_general | solution.py:57
  111.1 5.5 %fusion.25 = bf16[2048,256]{1,0:T(8,128)(2,1)S(1)} fusion(f32[2048,256]{1,0:T(8,128)S(1)} %fusion.4, bf16[1024,1024]{1,0:T(8,128)(2,1)S(1)} %get-tuple-element.87, bf16[1024,1024]{1,0:T(8,128)(2,1)S(1)} %copy-done.5, s32[256]{0:T(256)S(1)} %subtract_abs_fusion.1, s32[1024]{0:T(1024)S(1)} %subtract_abs_fusion, bf16[2048,256]{1,0:T(8,128)(2,1)S(1)} %fusion.23), kind=kOutput, calls=%fused_computation.51 | convolution fusion | flops 1088684032 | bytes 8393728 | tf_op jit(solution)/shard_map/while/body/eval_jaxpr/dot_general | solution.py:57
  117.7 4.9 %all-to-all-start.3 = ((bf16[4,256,256]{1,2,0:T(8,128)(2,1)}), bf16[4,256,256]{1,2,0:T(8,128)(2,1)S(1)}, u32[]{:S(2)}, u32[]{:S(2)}) async-start(bf16[4,256,256]{1,2,0:T(8,128)(2,1)} %copy.13), calls=%async_computation.3 | async-start | bytes 1048576 | tf_op jit(solution)/shard_map/while/body/eval_jaxpr/all_to_all | solution.py:124
  123.6 5.6 %all-to-all-done.3 = bf16[4,256,256]{1,2,0:T(8,128)(2,1)S(1)} async-done(((bf16[4,256,256]{1,2,0:T(8,128)(2,1)}), bf16[4,256,256]{1,2,0:T(8,128)(2,1)S(1)}, u32[]{:S(2)}, u32[]{:S(2)}) %all-to-all-start.3) | async-done | bytes 524320 | tf_op jit(solution)/shard_map/while/body/eval_jaxpr/all_to_all | solution.py:124
  129.2 4.9 %all-to-all-start.2 = ((bf16[4,256,256]{1,2,0:T(8,128)(2,1)}), bf16[4,256,256]{1,2,0:T(8,128)(2,1)S(1)}, u32[]{:S(2)}, u32[]{:S(2)}) async-start(bf16[4,256,256]{1,2,0:T(8,128)(2,1)} %copy.12), calls=%async_computation.2 | async-start | bytes 1048576 | tf_op jit(solution)/shard_map/while/body/eval_jaxpr/all_to_all | solution.py:123
  145.9 56.1 %all-reduce.4.cloned.1.call-done = bf16[256,1024]{1,0:T(8,128)(2,1)} async-done(((bf16[256,1024]{1,0:T(8,128)(2,1)}), bf16[256,1024]{1,0:T(8,128)(2,1)}) %all-reduce.4.cloned.1.call-update) | async-done | bytes 524304 | tf_op jit(solution)/shard_map/psum | solution.py:131
  202.0 4.5 fusion.1
  209.3 4.8 %all-to-all-start.5 = ((bf16[256,4,256]{2,0,1:T(8,128)(2,1)}), bf16[256,4,256]{2,0,1:T(8,128)(2,1)S(1)}, u32[]{:S(2)}, u32[]{:S(2)}) async-start(bf16[256,4,256]{2,0,1:T(8,128)(2,1)} %bitcast.76), calls=%async_computation.5 | async-start | bytes 1048576 | tf_op jit(solution)/shard_map/while/body/eval_jaxpr/all_to_all | solution.py:147
  215.0 6.6 %all-to-all-done.5 = bf16[256,4,256]{2,0,1:T(8,128)(2,1)S(1)} async-done(((bf16[256,4,256]{2,0,1:T(8,128)(2,1)}), bf16[256,4,256]{2,0,1:T(8,128)(2,1)S(1)}, u32[]{:S(2)}, u32[]{:S(2)}) %all-to-all-start.5) | async-done | bytes 524320 | tf_op jit(solution)/shard_map/while/body/eval_jaxpr/all_to_all | solution.py:147
  221.5 14.9 %all-to-all-start.4 = ((bf16[256,4,256]{2,0,1:T(8,128)(2,1)}), bf16[256,4,256]{2,0,1:T(8,128)(2,1)S(1)}, u32[]{:S(2)}, u32[]{:S(2)}) async-start(bf16[256,4,256]{2,0,1:T(8,128)(2,1)} %bitcast.77), calls=%async_computation.4 | async-start | bytes 1048576 | tf_op jit(solution)/shard_map/while/body/eval_jaxpr/all_to_all | solution.py:146
  244.4 4.9 %fusion.47 = f32[1024,256]{1,0:T(8,128)S(1)} fusion(bf16[512,1024]{1,0:T(8,128)(2,1)S(1)} %copy-done.15, bf16[512,1024]{1,0:T(8,128)(2,1)S(1)} %copy-done.10, f32[2048,256]{1,0:T(8,128)S(1)} %fusion.19, s32[256]{0:T(256)S(1)} %subtract_abs_fusion.1, s32[1024]{0:T(1024)S(1)} %subtract_abs_fusion), kind=kOutput, calls=%fused_computation.74 | convolution fusion | flops 546045952 | bytes 5248000 | tf_op jit(solution)/shard_map/dot_general | solution.py:57
  249.3 4.9 %fusion.66 = bf16[1024,256]{1,0:T(8,128)(2,1)S(1)} fusion(f32[1024,256]{1,0:T(8,128)S(1)} %fusion.47, bf16[512,1024]{1,0:T(8,128)(2,1)S(1)} %copy-done.10, bf16[512,1024]{1,0:T(8,128)(2,1)S(1)} %copy-done.12, f32[2048,256]{1,0:T(8,128)S(1)} %fusion.19, s32[256]{0:T(256)S(1)} %subtract_abs_fusion.1, s32[1024]{0:T(1024)S(1)} %subtract_abs_fusion), kind=kOutput, calls=%fused_computation.102 | convolution fusion | flops 546570240 | bytes 5772288 | tf_op jit(solution)/shard_map/dot_general | solution.py:57
  255.1 4.8 %all-to-all-start.6 = ((bf16[4,128,256]{1,2,0:T(8,128)(2,1)}), bf16[4,128,256]{1,2,0:T(8,128)(2,1)}, u32[]{:S(2)}, u32[]{:S(2)}) async-start(bf16[4,128,256]{1,2,0:T(8,128)(2,1)} %copy.16), calls=%async_computation.6 | async-start | bytes 524288 | tf_op jit(solution)/shard_map/all_to_all | solution.py:158
  260.8 4.5 all-to-all-done.6
  265.2 5.5 %all-to-all-start.7 = ((bf16[4,128,256]{1,2,0:T(8,128)(2,1)}), bf16[4,128,256]{1,2,0:T(8,128)(2,1)}, u32[]{:S(2)}, u32[]{:S(2)}) async-start(bf16[4,128,256]{1,2,0:T(8,128)(2,1)} %copy.17), calls=%async_computation.7 | async-start | bytes 524288 | tf_op jit(solution)/shard_map/all_to_all | solution.py:159
  280.4 178.5 %all-reduce.6.cloned.1.call-done = (f32[128,512]{1,0:T(8,128)}, f32[128,512]{1,0:T(8,128)}) async-done(((f32[128,512]{1,0:T(8,128)}, f32[128,512]{1,0:T(8,128)}), (f32[128,512]{1,0:T(8,128)}, f32[128,512]{1,0:T(8,128)})) %all-reduce.6.cloned.1.call-update) | async-done | bytes 524304 | tf_op jit(solution)/shard_map/psum | solution.py:164
  (108 shorter events, 54.0 us)
Async XLA Ops:
  7.2 17.5 %copy-start.19 = (f32[1,128,512]{2,1,0:T(8,128)S(1)}, f32[1,128,512]{2,1,0:T(8,128)}, u32[]{:S(2)}) copy-start(f32[1,128,512]{2,1,0:T(8,128)} %param.10) | copy-start | bytes 786436
  7.2 17.5 %copy-start.28 = (f32[128,512]{1,0:T(8,128)S(1)}, f32[128,512]{1,0:T(8,128)}, u32[]{:S(2)}) copy-start(f32[128,512]{1,0:T(8,128)} %param.7) | copy-start | bytes 786436
  7.2 17.5 %copy-start.16 = (s32[128,512]{1,0:T(8,128)S(1)}, s32[128,512]{1,0:T(8,128)}, u32[]{:S(2)}) copy-start(s32[128,512]{1,0:T(8,128)} %param.8) | copy-start | bytes 786436
  7.2 17.5 %copy-start.17 = (f32[128,512]{1,0:T(8,128)S(1)}, f32[128,512]{1,0:T(8,128)}, u32[]{:S(2)}) copy-start(f32[128,512]{1,0:T(8,128)} %param.9) | copy-start | bytes 786436
  16.2 10.0 %copy-start.11 = (bf16[512,1024]{1,0:T(8,128)(2,1)}, bf16[512,1024]{1,0:T(8,128)(2,1)S(1)}, u32[]{:S(2)}) copy-start(bf16[512,1024]{1,0:T(8,128)(2,1)S(1)} %get-tuple-element.85) | copy-start | bytes 3145732
  16.2 10.0 %copy-start.9 = (bf16[512,1024]{1,0:T(8,128)(2,1)}, bf16[512,1024]{1,0:T(8,128)(2,1)S(1)}, u32[]{:S(2)}) copy-start(bf16[512,1024]{1,0:T(8,128)(2,1)S(1)} %get-tuple-element.84) | copy-start | bytes 3145732
  28.2 64.4 %all-to-all-start = ((bf16[128,4,256]{2,0,1:T(8,128)(2,1)}), bf16[128,4,256]{2,0,1:T(8,128)(2,1)}, u32[]{:S(2)}, u32[]{:S(2)}) async-start(bf16[128,4,256]{2,0,1:T(8,128)(2,1)} %bitcast.79), calls=%async_computation | async-start | bytes 524288 | tf_op jit(solution)/shard_map/all_to_all | solution.py:113
  44.2 58.6 %copy-start.6 = (bf16[1024,512]{1,0:T(8,128)(2,1)}, bf16[1024,512]{1,0:T(8,128)(2,1)S(1)}, u32[]{:S(2)}) copy-start(bf16[1024,512]{1,0:T(8,128)(2,1)S(1)} %get-tuple-element.82) | copy-start | bytes 3145732
  72.2 61.9 %copy-start = (bf16[1024,1024]{1,0:T(8,128)(2,1)}, bf16[1024,1024]{1,0:T(8,128)(2,1)S(1)}, u32[]{:S(2)}) copy-start(bf16[1024,1024]{1,0:T(8,128)(2,1)S(1)} %get-tuple-element.87) | copy-start | bytes 6291460
  72.3 17.7 %copy-start.25 = (bf16[128,1024]{1,0:T(8,128)(2,1)S(1)}, bf16[128,1024]{1,0:T(8,128)(2,1)}, u32[]{:S(2)}) copy-start(bf16[128,1024]{1,0:T(8,128)(2,1)} %get-tuple-element.80) | copy-start | bytes 786436
  72.3 18.5 %copy-start.29 = (s32[1,2]{1,0:T(1,128)S(1)}, s32[1,2]{1,0:T(1,128)}, u32[]{:S(2)}) copy-start(s32[1,2]{1,0:T(1,128)} %param.11) | copy-start | bytes 28
  92.6 10.1 %all-to-all-start.1 = ((bf16[128,4,256]{2,0,1:T(8,128)(2,1)}), bf16[128,4,256]{2,0,1:T(8,128)(2,1)}, u32[]{:S(2)}, u32[]{:S(2)}) async-start(bf16[128,4,256]{2,0,1:T(8,128)(2,1)} %bitcast.84), calls=%async_computation.1 | async-start | bytes 524288 | tf_op jit(solution)/shard_map/all_to_all | solution.py:114
  117.7 11.5 %all-to-all-start.3 = ((bf16[4,256,256]{1,2,0:T(8,128)(2,1)}), bf16[4,256,256]{1,2,0:T(8,128)(2,1)S(1)}, u32[]{:S(2)}, u32[]{:S(2)}) async-start(bf16[4,256,256]{1,2,0:T(8,128)(2,1)} %copy.13), calls=%async_computation.3 | async-start | bytes 1048576 | tf_op jit(solution)/shard_map/while/body/eval_jaxpr/all_to_all | solution.py:124
  129.2 11.5 %all-to-all-start.2 = ((bf16[4,256,256]{1,2,0:T(8,128)(2,1)}), bf16[4,256,256]{1,2,0:T(8,128)(2,1)S(1)}, u32[]{:S(2)}, u32[]{:S(2)}) async-start(bf16[4,256,256]{1,2,0:T(8,128)(2,1)} %copy.12), calls=%async_computation.2 | async-start | bytes 1048576 | tf_op jit(solution)/shard_map/while/body/eval_jaxpr/all_to_all | solution.py:123
  134.1 67.9 %all-reduce.4.cloned.1.call-start = ((), (), s32[]{:S(2)}) async-start(), calls=%async_computation.8 | async-start | bytes 1048576 | tf_op jit(solution)/shard_map/psum | solution.py:131
  208.5 28.0 %copy-start.2 = (bf16[1024,1024]{1,0:T(8,128)(2,1)S(1)}, bf16[1024,1024]{1,0:T(8,128)(2,1)}, u32[]{:S(2)}) copy-start(bf16[1024,1024]{1,0:T(8,128)(2,1)} %copy-done) | copy-start | bytes 6291460
  209.3 12.2 %all-to-all-start.5 = ((bf16[256,4,256]{2,0,1:T(8,128)(2,1)}), bf16[256,4,256]{2,0,1:T(8,128)(2,1)S(1)}, u32[]{:S(2)}, u32[]{:S(2)}) async-start(bf16[256,4,256]{2,0,1:T(8,128)(2,1)} %bitcast.76), calls=%async_computation.5 | async-start | bytes 1048576 | tf_op jit(solution)/shard_map/while/body/eval_jaxpr/all_to_all | solution.py:147
  221.5 19.1 %all-to-all-start.4 = ((bf16[256,4,256]{2,0,1:T(8,128)(2,1)}), bf16[256,4,256]{2,0,1:T(8,128)(2,1)S(1)}, u32[]{:S(2)}, u32[]{:S(2)}) async-start(bf16[256,4,256]{2,0,1:T(8,128)(2,1)} %bitcast.77), calls=%async_computation.4 | async-start | bytes 1048576 | tf_op jit(solution)/shard_map/while/body/eval_jaxpr/all_to_all | solution.py:146
  254.2 16.5 %copy-start.7 = (bf16[1024,512]{1,0:T(8,128)(2,1)S(1)}, bf16[1024,512]{1,0:T(8,128)(2,1)}, u32[]{:S(2)}) copy-start(bf16[1024,512]{1,0:T(8,128)(2,1)} %copy-done.6) | copy-start | bytes 3145732
  254.2 16.5 %copy-start.13 = (bf16[1024,512]{1,0:T(8,128)(2,1)S(1)}, bf16[1024,512]{1,0:T(8,128)(2,1)}, u32[]{:S(2)}) copy-start(bf16[1024,512]{1,0:T(8,128)(2,1)} %fusion.97) | copy-start | bytes 3145732
  255.1 10.1 %all-to-all-start.6 = ((bf16[4,128,256]{1,2,0:T(8,128)(2,1)}), bf16[4,128,256]{1,2,0:T(8,128)(2,1)}, u32[]{:S(2)}, u32[]{:S(2)}) async-start(bf16[4,128,256]{1,2,0:T(8,128)(2,1)} %copy.16), calls=%async_computation.6 | async-start | bytes 524288 | tf_op jit(solution)/shard_map/all_to_all | solution.py:158
  260.7 15.3 %copy-start.8 = (bf16[1024,512]{1,0:T(8,128)(2,1)S(1)}, bf16[1024,512]{1,0:T(8,128)(2,1)}, u32[]{:S(2)}) copy-start(bf16[1024,512]{1,0:T(8,128)(2,1)} %get-tuple-element.83) | copy-start | bytes 3145732
  265.2 10.8 %all-to-all-start.7 = ((bf16[4,128,256]{1,2,0:T(8,128)(2,1)}), bf16[4,128,256]{1,2,0:T(8,128)(2,1)}, u32[]{:S(2)}, u32[]{:S(2)}) async-start(bf16[4,128,256]{1,2,0:T(8,128)(2,1)} %copy.17), calls=%async_computation.7 | async-start | bytes 524288 | tf_op jit(solution)/shard_map/all_to_all | solution.py:159
  270.7 188.2 %all-reduce.6.cloned.1.call-start = ((), (), s32[]{:S(2)}) async-start(), calls=%async_computation.9 | async-start | bytes 1048576 | tf_op jit(solution)/shard_map/psum | solution.py:164
  (18 other events, 67.8 us)
Sparse Core Ops, SparseCore 0:
  146.0 55.9 all-reduce.3
  279.6 179.2 all-reduce.5
where the time goes:
time: 478 us; the launch traced here: 469 us
  waiting for transfers between devices  258 us (54%)
  other arithmetic  78.1 us (16%)
  matrix products  53.8 us (11%)
  starting transfers between devices  51.1 us (11%)
  between operations  14.7 us (3%)
  local copies, waits for them, and re-layouts  13.1 us (3%)
    psum x1, waiting for transfers between devices, shards(): lax.psum((phase_sum / frame_total, amp_sum / frame_total), ('frame', 'mod'))  178 us
    psum x1, waiting for transfers between devices, shards(): lax.psum(running.astype(jnp.bfloat16), 'mod').astype(jnp.float32)  56.1 us
    neg x2, other arithmetic, left_blocks(): -imag_part  26.9 us
    convert_element_type x1, other arithmetic, to_bfloat(): complex_pair[1].astype(jnp.bfloat16)  18.9 us
    convert_element_type x2, other arithmetic, to_bfloat(): complex_pair[0].astype(jnp.bfloat16)  18.7 us
    dot_general x4, matrix products, left_product(): jnp.dot(blocks[0], field_pair[0], preferred_element_type=jnp.float32)  17.5 us
    dot_general x4, matrix products, left_product(): jnp.dot(blocks[1], field_pair[1], preferred_element_type=jnp.float32)  17.4 us
    all_to_all x1, starting transfers between devices, adjoint(): lax.all_to_all(inner_pass[0], 'row', split_axis=1, concat_axis=0, tiled=T...  14.9 us
  transfers between devices with their start and end apart: 10, of which 8 were waited for; matrix products, arithmetic and copies ran while one was open for 16% of the time, Pallas kernels for 0%

commit v1 on v0

v1 whole, which is shorter than its diff:
```python
import functools
import math

import jax
import jax.numpy as jnp
from jax import lax
from jax.experimental import pallas as pl
from jax.experimental.pallas import tpu as pltpu
from jax.sharding import Mesh
from jax.sharding import PartitionSpec as P

BF = jnp.bfloat16
F32 = jnp.float32
PUPIL = 512
FULL = 1024
ROWS = 256
COLS = 512
BLOCK = 128
VMEM = pltpu.VMEM
SMEM = pltpu.SMEM


def sincos(angle):
    turns = jnp.floor(angle * (2.0 / math.pi) + 0.5)
    rest = angle - turns * 1.5703125
    rest = rest - turns * 4.837512969970703125e-4
    rest = rest - turns * 7.549789954891882e-8
    quadrant = turns.astype(jnp.int32)
    square = rest * rest
    sine = rest + rest * square * (
        -1.6666654611e-1 + square * (8.3321608736e-3 + square * -1.9515295891e-4)
    )
    cosine = (
        1.0
        - 0.5 * square
        + square
        * square
        * (4.166664568298827e-2 + square * (-1.388731625493765e-3 + square * 2.443315711809948e-5))
    )
    odd = (quadrant & 1) == 1
    sin_out = jnp.where(odd, cosine, sine)
    cos_out = jnp.where(odd, sine, cosine)
    sin_out = jnp.where((quadrant & 2) != 0, -sin_out, sin_out)
    cos_out = jnp.where(((quadrant + 1) & 2) != 0, -cos_out, cos_out)
    return sin_out, cos_out


def unit_sincos(steps):
    return sincos((steps & (2 * FULL - 1)).astype(F32) * (math.pi / FULL))


def dot(left, right):
    return jnp.dot(left, right, preferred_element_type=F32)


def dot_t(left, right):
    return lax.dot_general(left, right, (((1,), (1,)), ((), ())), preferred_element_type=F32)


def response(lag, offset):
    count_up = FULL // 2 - offset
    count_down = FULL // 2 + offset
    step_up = (lag + FULL // 4) & (FULL - 1)
    step_down = (FULL // 4 - lag) & (FULL - 1)
    shift = 2 * lag * offset

    def ratio(step, count):
        over, _ = unit_sincos(step * count)
        under, _ = unit_sincos(step)
        flat = step == 0
        return jnp.where(flat, count.astype(F32), over / jnp.where(flat, 1.0, under))

    size_up = ratio(step_up, count_up) * (1.0 / FULL)
    size_down = ratio(step_down, count_down) * (1.0 / FULL)
    sin_up, cos_up = unit_sincos((count_up - 1) * step_up + shift)
    sin_down, cos_down = unit_sincos((count_down + 1) * step_down + shift)
    return size_up * cos_up + size_down * cos_down, size_up * sin_up + size_down * sin_down


def field_kernel(amp_ref, mask_ref, phase_ref, screen_ref, out_ref):
    sine, cosine = sincos(phase_ref[...] + screen_ref[...])
    weight = amp_ref[...] * mask_ref[...].astype(F32)
    out_ref[:, :PUPIL] = (weight * cosine).astype(BF)
    out_ref[:, PUPIL:] = (weight * sine).astype(BF)


def table_kernel(place_ref, offset_ref, left_ref, back_ref, right_ref, strip_ref):
    row_at = place_ref[0]
    mod_at = place_ref[1]
    lane = lax.broadcasted_iota(jnp.int32, (8, FULL), 1)

    def strips(parts):
        for part in range(2):
            base = pltpu.roll(parts[part], 0, 1, stride=1, stride_axis=0)
            for group in range(0, BLOCK, 16):
                low = pltpu.roll(base, group, 1) if group else base
                high = pltpu.roll(base, group + 8, 1)
                strip_ref[part, pl.ds(group, 16), :] = jnp.concatenate([low, high], axis=0).astype(BF)

    def window(part, blocks):
        start = pl.multiple_of((blocks & 7) * BLOCK, BLOCK)
        return strip_ref[part, :, pl.ds(start, BLOCK)]

    def each(count):
        return [(part, i, k) for part in range(2) for i in range(count[0]) for k in range(count[1])]

    row_offset = offset_ref[0, 0]
    strips(response(-lane - FULL // 4, row_offset))
    for part, i, d in each((ROWS // BLOCK, 4)):
        left_ref[part, pl.ds(i * BLOCK, BLOCK), pl.ds(d * BLOCK, BLOCK)] = window(
            part, ((row_at + d) & 3) - 2 * row_at - i
        )
    strips(response(lane - FULL // 4, row_offset))
    for part, d, i in each((4, ROWS // BLOCK)):
        back_ref[part, pl.ds(d * BLOCK, BLOCK), pl.ds(i * BLOCK, BLOCK)] = window(
            part, 2 * row_at + i - ((row_at + d) & 3)
        )
    strips(response(-lane - FULL // 4, offset_ref[0, 1]))
    for part, i, k in each((4, 4)):
        right_ref[part, pl.ds(i * BLOCK, BLOCK), pl.ds(k * BLOCK, BLOCK)] = window(
            part, k - 4 * mod_at - i
        )


def detector_kernel(
    left_a, left_b, right_a, right_b, e0, e1, e2, e3, measured_ref, valid_ref, image_ref, back_ref,
    pupil_ref, half_ref, det_ref, weighted_ref,
):
    for d, block in enumerate((e0, e1, e2, e3)):
        pupil_ref[pl.ds(d * BLOCK, BLOCK), :] = block[...]
    lefts, rights = (left_a, left_b), (right_a, right_b)
    wide = 256
    for m in range(2):
        for at in range(0, PUPIL, wide):
            real = pupil_ref[:, pl.ds(at, wide)]
            imag = pupil_ref[:, pl.ds(PUPIL + at, wide)]
            half_ref[m, :, pl.ds(at, wide)] = (
                dot(lefts[m][0], real) - dot(lefts[m][1], imag)
            ).astype(BF)
            half_ref[m, :, pl.ds(PUPIL + at, wide)] = (
                dot(lefts[m][0], imag) + dot(lefts[m][1], real)
            ).astype(BF)
    for at in range(0, COLS, wide):
        total = None
        for m in range(2):
            real = rights[m][0, pl.ds(at, wide), :]
            imag = rights[m][1, pl.ds(at, wide), :]
            half_real = half_ref[m, :, :PUPIL]
            half_imag = half_ref[m, :, PUPIL:]
            det_real = dot_t(half_real, real) - dot_t(half_imag, imag)
            det_imag = dot_t(half_real, imag) + dot_t(half_imag, real)
            det_ref[m, 0] = det_real
            det_ref[m, 1] = det_imag
            power = det_real * det_real + det_imag * det_imag
            total = power if total is None else total + power
        image = 0.5 * total
        image_ref[:, pl.ds(at, wide)] = image
        residual = valid_ref[:, pl.ds(at, wide)].astype(F32) * (
            image - measured_ref[:, pl.ds(at, wide)]
        )
        for m in range(2):
            for part in range(2):
                weighted_ref[m, part, :, pl.ds(at, wide)] = (residual * det_ref[m, part]).astype(BF)
    for m in range(2):
        real_in = weighted_ref[m, 0]
        imag_in = weighted_ref[m, 1]
        for at in range(0, PUPIL, wide):
            real = rights[m][0, :, pl.ds(at, wide)]
            imag = rights[m][1, :, pl.ds(at, wide)]
            back_ref[m, :, pl.ds(at, wide)] = (dot(real_in, real) + dot(imag_in, imag)).astype(BF)
            back_ref[m, :, pl.ds(PUPIL + at, wide)] = (
                dot(imag_in, real) - dot(real_in, imag)
            ).astype(BF)


def gradient_kernel(d, back_a, back_b, half_ref, pupil_ref, out_ref):
    backs = (back_a, back_b)
    wide = 256
    here = pl.ds(d * BLOCK, BLOCK)
    for at in range(0, PUPIL, wide):
        real = imag = None
        for m in range(2):
            half_real = half_ref[m, :, pl.ds(at, wide)]
            half_imag = half_ref[m, :, pl.ds(PUPIL + at, wide)]
            table_real = backs[m][0, here, :]
            table_imag = backs[m][1, here, :]
            more_real = dot(table_real, half_real) + dot(table_imag, half_imag)
            more_imag = dot(table_real, half_imag) - dot(table_imag, half_real)
            real = more_real if real is None else real + more_real
            imag = more_imag if imag is None else imag + more_imag
        field_real = pupil_ref[:, pl.ds(at, wide)].astype(F32)
        field_imag = pupil_ref[:, pl.ds(PUPIL + at, wide)].astype(F32)
        out_ref[:, pl.ds(at, wide)] = (real * field_real + imag * field_imag).astype(BF)
        out_ref[:, pl.ds(PUPIL + at, wide)] = (imag * field_real - real * field_imag).astype(BF)


TILE = 16
PIECES = BLOCK * PUPIL // (TILE * 128)


def fold_kernel(core_ref, s0, s1, s2, s3, keep_ref, send_ref):
    first = core_ref[0] == 0
    for k in range(4):
        for r in range(BLOCK // TILE):
            rows = pl.ds(r * TILE, TILE)
            sums = []
            for part in range(2):
                at = pl.ds(part * PUPIL + k * 128, 128)
                sums.append(
                    s0[rows, at].astype(F32)
                    + s1[rows, at].astype(F32)
                    + s2[rows, at].astype(F32)
                    + s3[rows, at].astype(F32)
                )
            piece = k * (BLOCK // TILE) + r
            keep_ref[piece] = jnp.where(first, sums[0], sums[1]).astype(BF)
            send_ref[piece] = jnp.where(first, sums[1], sums[0]).astype(BF)


def spread_kernel(got_ref, out_ref):
    total = jnp.sum(got_ref[...].astype(F32), axis=0).astype(BF)
    out_ref[...] = jnp.broadcast_to(total[None], out_ref.shape)


def finish_kernel(frames, core_ref, own_ref, other_ref, amp_ref, phase_out, amp_out):
    first = core_ref[0] == 0
    for k in range(4):
        for r in range(BLOCK // TILE):
            rows, at = pl.ds(r * TILE, TILE), pl.ds(k * 128, 128)
            piece = k * (BLOCK // TILE) + r
            own = own_ref[piece].astype(F32)
            other = other_ref[piece].astype(F32)
            amp_out[rows, at] = jnp.where(first, own, other) / (frames * amp_ref[rows, at])
            phase_out[rows, at] = jnp.where(first, other, own) * (1.0 / frames)


def struct(shape, dtype):
    return jax.ShapeDtypeStruct(shape, dtype)


def call(kernel, outs, scalars, vectors, scratch=(), flops=0):
    specs = [pl.BlockSpec(memory_space=SMEM)] * len(scalars) + [
        pl.BlockSpec(memory_space=VMEM)
    ] * len(vectors)
    moved = sum(math.prod(v.shape) * v.dtype.itemsize for v in vectors)
    return pl.pallas_call(
        kernel,
        out_shape=outs,
        in_specs=specs,
        out_specs=jax.tree.map(lambda _: pl.BlockSpec(memory_space=VMEM), outs),
        scratch_shapes=list(scratch),
        cost_estimate=pl.CostEstimate(flops=flops, bytes_accessed=moved, transcendentals=0),
    )(*scalars, *vectors)


def tables(place, offset_pair):
    return call(
        table_kernel,
        [
            struct((2, ROWS, PUPIL), BF),
            struct((2, PUPIL, ROWS), BF),
            struct((2, COLS, PUPIL), BF),
        ],
        (place, offset_pair),
        (),
        [VMEM((2, BLOCK, FULL), BF)],
        flops=4_000_000,
    )


def detector(left_a, left_b, right_a, right_b, fields, target, live):
    return call(
        detector_kernel,
        [struct((ROWS, COLS), F32), struct((2, ROWS, 2 * PUPIL), BF)],
        (),
        (left_a, left_b, right_a, right_b, *fields, target, live),
        [
            VMEM((PUPIL, 2 * PUPIL), BF),
            VMEM((2, ROWS, 2 * PUPIL), BF),
            VMEM((2, 2, ROWS, 256), F32),
            VMEM((2, 2, ROWS, COLS), BF),
        ],
        flops=3_221_000_000,
    )


def gradient(d, back_a, back_b, half, field):
    return call(
        functools.partial(gradient_kernel, d),
        struct((BLOCK, 2 * PUPIL), BF),
        (),
        (back_a, back_b, half, field),
        flops=268_000_000,
    )


def shards(amplitude, pupil_mask, phase_common, screens, offsets, measured, valid):
    row_at = lax.axis_index("x")
    mod_at = lax.axis_index("zh")
    core = lax.axis_index("core").astype(jnp.int32).reshape(1)
    place = jnp.stack([row_at, mod_at]).astype(jnp.int32)
    ring = lambda d: [(i, (i + d) % 4) for i in range(4)]
    swap = [(0, 1), (1, 0)]
    frames = 32

    field = call(
        field_kernel,
        struct((BLOCK, 2 * PUPIL), BF),
        (),
        (amplitude, pupil_mask, phase_common, screens[0]),
    )
    fields = [field] + [lax.ppermute(field, "x", ring(-d)) for d in (1, 2, 3)]
    offsets_b = lax.ppermute(offsets, "zh", swap)
    left_a, back_a, right_a = tables(place, offsets)
    left_b, back_b, right_b = tables(place, offsets_b)
    target = lax.dynamic_slice_in_dim(measured[0], mod_at * COLS, COLS, 1)
    live = lax.dynamic_slice_in_dim(valid, mod_at * COLS, COLS, 1)
    image, half = detector(left_a, left_b, right_a, right_b, fields, target, live)
    arrived = []
    for d in (2, 1, 3):
        part = gradient(d, back_a, back_b, half, fields[d])
        arrived.append(lax.ppermute(part, "x", ring(d)))
    own = gradient(0, back_a, back_b, half, fields[0])
    keep, send = call(
        fold_kernel, [struct((PIECES, TILE, 128), BF)] * 2, (core,), (own, *arrived)
    )
    keep = (keep.astype(F32) + lax.ppermute(send, "core", swap).astype(F32)).astype(BF)
    around = ("y", "zh", "zl")
    got = lax.all_to_all(keep, around, 0, 0)
    spread = call(spread_kernel, struct((PIECES, TILE, 128), BF), (), (got,))
    mine = lax.all_to_all(spread, around, 0, 0)
    other = lax.ppermute(mine, "core", swap)
    phase_grad, amp_grad = call(
        functools.partial(finish_kernel, frames),
        [struct((BLOCK, PUPIL), F32)] * 2,
        (core,),
        (mine, other, amplitude),
    )
    return image[None], phase_grad, amp_grad


def solution(mesh):
    fine = Mesh(mesh.devices.reshape(4, 4, 2, 2, 4), ("zl", "y", "core", "zh", "x"))
    frame = ("zl", "y", "core")
    rows = P("x", None)
    return jax.shard_map(
        shards,
        mesh=fine,
        in_specs=(
            rows, rows, rows, P(frame, "x", None), P("zh", None), P(frame, "x", None), rows
        ),
        out_specs=(P(frame, "x", "zh"), rows, rows),
        check_vma=False,
    )
```

time: 478 us -> 95.2 us (0.20); the launches traced: 469 us -> 93.4 us
  waiting for transfers between devices: 258 us -> 6.71 us
  other arithmetic: 78.1 us -> 1.61 us
  matrix products: 53.8 us -> 0 us
  starting transfers between devices: 51.1 us -> 14.8 us
  Pallas kernels: 0 us -> 34 us
  blocking collectives: 0 us -> 31 us
  between operations: 14.7 us -> 0.71 us
  local copies, waits for them, and re-layouts: 13.1 us -> 4.43 us
    psum x2 -> x0, waiting for transfers between devices: 235 us -> none  [the longest x1 178 us: shards(): lax.psum((phase_sum / frame_total, amp_sum / frame_total), ('frame', 'mod'))]
    dot_general x16 -> x0, matrix products: 53.8 us -> none  [the longest x4 17.5 us: left_product(): jnp.dot(blocks[0], field_pair[0], preferred_element_type=jnp.float32)]
    all_to_all x8 -> x0, starting transfers between devices: 51.1 us -> none  [the longest x1 14.9 us: adjoint(): lax.all_to_all(inner_pass[0], 'row', split_axis=1, concat_axis=0, tiled=T...]
    convert_element_type x4 -> x1, other arithmetic: 38.6 us -> 0.95 us  [shards(): (keep.astype(F32) + lax.ppermute(send, 'core', swap).astype(F32)).astype(BF)]
    neg x3 -> x0, other arithmetic: 35.3 us -> none  [the longest x2 26.9 us: left_blocks(): -imag_part]
    pallas_call x0 -> x11, Pallas kernels: none -> 34 us  [call(): pl.pallas_call(kernel, out_shape=outs, in_specs=specs, out_specs=jax.tree...]
    all_to_all x0 -> x2, blocking collectives: none -> 31 us  [the longest x1 16.8 us: shards(): got = lax.all_to_all(keep, around, 0, 0)]
    all_to_all x8 -> x0, waiting for transfers between devices: 23.9 us -> none  [the longest x1 6.56 us: adjoint(): lax.all_to_all(inner_pass[1], 'row', split_axis=1, concat_axis=0, tiled=T...]
  transfers between devices with their start and end apart: 10 -> 9, of which waited for: 8 -> 4; matrix products, arithmetic and copies ran while one was open for 16% -> 3% of each run, Pallas kernels for 0% -> 17%
where the time goes in v1:
time: 95.2 us; the launch traced here: 93.4 us
  Pallas kernels  34 us (36%)
  blocking collectives  31 us (33%)
  starting transfers between devices  14.8 us (16%)
  waiting for transfers between devices  6.71 us (7%)
  local copies, waits for them, and re-layouts  4.43 us (5%)
  other arithmetic  1.61 us (2%)
    pallas_call x11, Pallas kernels, call(): pl.pallas_call(kernel, out_shape=outs, in_specs=specs, out_specs=jax.tree...  34 us
    all_to_all x1, blocking collectives, shards(): got = lax.all_to_all(keep, around, 0, 0)  16.8 us
    all_to_all x1, blocking collectives, shards(): mine = lax.all_to_all(spread, around, 0, 0)  14.3 us
    ppermute x1, starting transfers between devices, shards(): offsets_b = lax.ppermute(offsets, 'zh', swap)  7.19 us
    ppermute x3, starting transfers between devices, shards(): fields = [field] + [lax.ppermute(field, 'x', ring(-d)) for d in (1, 2, 3)]  4.76 us
    ppermute x3, waiting for transfers between devices, shards(): arrived.append(lax.ppermute(part, 'x', ring(d)))  3.8 us
    ppermute x3, starting transfers between devices, shards(): arrived.append(lax.ppermute(part, 'x', ring(d)))  2.89 us
    unnamed x24, local copies, waits for them, and re-layouts  2.73 us
  transfers between devices with their start and end apart: 9, of which 4 were waited for; matrix products, arithmetic and copies ran while one was open for 3% of the time, Pallas kernels for 17%

profile of v1, /device:TPU:2, one launch (start us, length us, event | category | flops | bytes accessed | tf_op | source)
XLA Modules:
  0.0 93.4 jit_solution(3461349173559916192)
XLA Ops:
  0.7 2.5 %shard_map.96.e0.pupil_ref = bf16[128,1024]{1,0:T(8,128)(2,1)} custom-call(f32[128,512]{1,0:T(8,128)} %amp_ref.3, s32[128,512]{1,0:T(8,128)} %mask_ref.1, f32[128,512]{1,0:T(8,128)} %phase_ref.1, f32[128,512]{1,0:T(8,128)} %bitcast.7), custom_call_target="tpu_custom_call" | custom-call | bytes 1048576 | tf_op jit(solution)/shard_map/pallas_call | solution.py:246
  3.1 1.5 %collective-permute-start.3 = (bf16[128,1024]{1,0:T(8,128)(2,1)}, bf16[128,1024]{1,0:T(8,128)(2,1)S(1)}, u32[]{:S(2)}, u32[]{:S(2)}) collective-permute-start(bf16[128,1024]{1,0:T(8,128)(2,1)} %shard_map.96.e0.pupil_ref), channel_id=1, source_target_pairs={{0,1},{1,2},{2,3},{3,0},{4,5},{5,6},{6,7},{7,4},{8,9},{9,10},{10,1... | collective-permute-start | bytes 786440 | tf_op jit(solution)/shard_map/ppermute | solution.py:312
  4.6 2.8 %collective-permute-start.2 = (bf16[128,1024]{1,0:T(8,128)(2,1)}, bf16[128,1024]{1,0:T(8,128)(2,1)S(1)}, u32[]{:S(2)}, u32[]{:S(2)}) collective-permute-start(bf16[128,1024]{1,0:T(8,128)(2,1)} %shard_map.96.e0.pupil_ref), channel_id=1, source_target_pairs={{0,2},{1,3},{2,0},{3,1},{4,6},{5,7},{6,4},{7,5},{8,10},{9,11},{10,... | collective-permute-start | bytes 786440 | tf_op jit(solution)/shard_map/ppermute | solution.py:312
  7.9 7.2 %collective-permute-start = (s32[1,2]{1,0:T(1,128)S(1)}, s32[1,2]{1,0:T(1,128)S(1)}, u32[]{:S(2)}, u32[]{:S(2)}) collective-permute-start(s32[1,2]{1,0:T(1,128)S(1)} %copy-done.10), channel_id=1, source_target_pairs={{0,4},{4,0},{1,5},{5,1},{2,6},{6,2},{3,7},{7,3},{8,12},{12,8},{9,1... | collective-permute-start | bytes 32 | tf_op jit(solution)/shard_map/ppermute | solution.py:313
  15.7 3.8 %shard_map.94 = (bf16[2,256,512]{2,1,0:T(8,128)(2,1)}, bf16[2,512,256]{2,1,0:T(8,128)(2,1)}, bf16[2,512,512]{2,1,0:T(8,128)(2,1)}) custom-call(s32[2]{0:T(128)} %pad_add_fusion.place_ref, s32[1,2]{1,0:T(1,128)} %offset_ref.1), custom_call_target="tpu_custom_call" | custom-call | flops 4000000 | tf_op jit(solution)/shard_map/pallas_call | solution.py:246
  19.6 0.8 dynamic-slice_bitcast_fusion.measured_ref
  20.4 0.9 constant_dynamic-slice_fusion.valid_ref
  21.8 3.8 %shard_map.95 = (bf16[2,256,512]{2,1,0:T(8,128)(2,1)}, bf16[2,512,256]{2,1,0:T(8,128)(2,1)}, bf16[2,512,512]{2,1,0:T(8,128)(2,1)}) custom-call(s32[2]{0:T(128)} %pad_add_fusion.place_ref, s32[1,2]{1,0:T(1,128)} %copy-done.11), custom_call_target="tpu_custom_call" | custom-call | flops 4000000 | tf_op jit(solution)/shard_map/pallas_call | solution.py:246
  26.5 7.3 %shard_map.97 = (f32[256,512]{1,0:T(8,128)}, bf16[2,256,1024]{2,1,0:T(8,128)(2,1)}) custom-call(bf16[2,256,512]{2,1,0:T(8,128)(2,1)} %get-tuple-element.15.left_a, bf16[2,256,512]{2,1,0:T(8,128)(2,1)} %get-tuple-element.16.left_b, bf16[2,512,512]{2,1,0:T(8,128)(2,1)} %get-tuple-element.17.right_a, bf16[2,512,512]{2,1,0:T(8,128)(2,1)} %get-tuple-element.18.right_b, ...), custom_call_target="tpu_custom_call" | custom-call | flops 3220999936 | bytes 5242880 | tf_op jit(solution)/shard_map/pallas_call | solution.py:246
  33.7 2.8 %shard_map.99 = bf16[128,1024]{1,0:T(8,128)(2,1)} custom-call(bf16[2,512,256]{2,1,0:T(8,128)(2,1)} %get-tuple-element.20.back_a, bf16[2,512,256]{2,1,0:T(8,128)(2,1)} %get-tuple-element.21.back_b, bf16[2,256,1024]{2,1,0:T(8,128)(2,1)} %get-tuple-element.22.half_ref, bf16[128,1024]{1,0:T(8,128)(2,1)} %copy-done.4), custom_call_target="tpu_custom_call" | custom-call | flops 268000000 | bytes 2359296 | tf_op jit(solution)/shard_map/pallas_call | solution.py:246
  36.8 2.8 %shard_map.100 = bf16[128,1024]{1,0:T(8,128)(2,1)} custom-call(bf16[2,512,256]{2,1,0:T(8,128)(2,1)} %get-tuple-element.20.back_a, bf16[2,512,256]{2,1,0:T(8,128)(2,1)} %get-tuple-element.21.back_b, bf16[2,256,1024]{2,1,0:T(8,128)(2,1)} %get-tuple-element.22.half_ref, bf16[128,1024]{1,0:T(8,128)(2,1)} %copy-done.3), custom_call_target="tpu_custom_call" | custom-call | flops 268000000 | bytes 2359296 | tf_op jit(solution)/shard_map/pallas_call | solution.py:246
  39.6 2.6 %collective-permute-start.5 = (bf16[128,1024]{1,0:T(8,128)(2,1)}, bf16[128,1024]{1,0:T(8,128)(2,1)S(1)}, u32[]{:S(2)}, u32[]{:S(2)}) collective-permute-start(bf16[128,1024]{1,0:T(8,128)(2,1)} %shard_map.100), channel_id=1, source_target_pairs={{0,1},{1,2},{2,3},{3,0},{4,5},{5,6},{6,7},{7,4},{8,9},{9,10},{10,1... | collective-permute-start | bytes 786440 | tf_op jit(solution)/shard_map/ppermute | solution.py:322
  42.2 2.8 %shard_map.101 = bf16[128,1024]{1,0:T(8,128)(2,1)} custom-call(bf16[2,512,256]{2,1,0:T(8,128)(2,1)} %get-tuple-element.20.back_a, bf16[2,512,256]{2,1,0:T(8,128)(2,1)} %get-tuple-element.21.back_b, bf16[2,256,1024]{2,1,0:T(8,128)(2,1)} %get-tuple-element.22.half_ref, bf16[128,1024]{1,0:T(8,128)(2,1)} %copy-done.2), custom_call_target="tpu_custom_call" | custom-call | flops 268000000 | bytes 2359296 | tf_op jit(solution)/shard_map/pallas_call | solution.py:246
  44.9 2.8 %shard_map.98.s0 = bf16[128,1024]{1,0:T(8,128)(2,1)} custom-call(bf16[2,512,256]{2,1,0:T(8,128)(2,1)} %get-tuple-element.20.back_a, bf16[2,512,256]{2,1,0:T(8,128)(2,1)} %get-tuple-element.21.back_b, bf16[2,256,1024]{2,1,0:T(8,128)(2,1)} %get-tuple-element.22.half_ref, bf16[128,1024]{1,0:T(8,128)(2,1)} %shard_map.96.e0.pupil_ref), custom_call_target="tpu_custom_call" | custom-call | flops 268000000 | bytes 2359296 | tf_op jit(solution)/shard_map/pallas_call | solution.py:246
  47.7 1.4 %collective-permute-done.5.s2 = bf16[128,1024]{1,0:T(8,128)(2,1)S(1)} collective-permute-done((bf16[128,1024]{1,0:T(8,128)(2,1)}, bf16[128,1024]{1,0:T(8,128)(2,1)S(1)}, u32[]{:S(2)}, u32[]{:S(2)}) %collective-permute-start.5) | collective-permute-done | bytes 262176 | tf_op jit(solution)/shard_map/ppermute | solution.py:322
  49.2 2.4 %collective-permute-done.6.s3 = bf16[128,1024]{1,0:T(8,128)(2,1)S(1)} collective-permute-done((bf16[128,1024]{1,0:T(8,128)(2,1)}, bf16[128,1024]{1,0:T(8,128)(2,1)S(1)}, u32[]{:S(2)}, u32[]{:S(2)}) %collective-permute-start.6) | collective-permute-done | bytes 262176 | tf_op jit(solution)/shard_map/ppermute | solution.py:322
  52.2 2.0 %shard_map.102 = (bf16[32,16,128]{2,1,0:T(8,128)(2,1)}, bf16[32,16,128]{2,1,0:T(8,128)(2,1)}) custom-call(s32[1]{0:T(128)} %bitcast.5.core_ref, bf16[128,1024]{1,0:T(8,128)(2,1)} %shard_map.98.s0, bf16[128,1024]{1,0:T(8,128)(2,1)} %copy-done.6, bf16[128,1024]{1,0:T(8,128)(2,1)} %copy-done.7, bf16[128,1024]{1,0:T(8,128)(2,1)} %copy-done.8), custom_call_target="tpu_custom_call" | custom-call | bytes 1048576 | tf_op jit(solution)/shard_map/pallas_call | solution.py:246
  54.3 1.6 %collective-permute-done.7 = bf16[32,16,128]{2,1,0:T(8,128)(2,1)S(1)} collective-permute-done((bf16[32,16,128]{2,1,0:T(8,128)(2,1)}, bf16[32,16,128]{2,1,0:T(8,128)(2,1)S(1)}, u32[]{:S(2)}, u32[]{:S(2)}) %collective-permute-start.7) | collective-permute-done | bytes 131104 | tf_op jit(solution)/shard_map/ppermute | solution.py:327
  55.8 0.9 %add_convert_fusion = bf16[32,16,128]{2,1,0:T(8,128)(2,1)S(1)} fusion(bf16[32,16,128]{2,1,0:T(8,128)(2,1)S(1)} %collective-permute-done.7, bf16[32,16,128]{2,1,0:T(8,128)(2,1)} %get-tuple-element.23), kind=kLoop, calls=%fused_computation.1 | loop fusion | flops 262144 | bytes 393216 | tf_op jit(solution)/shard_map/convert_element_type | solution.py:327
  56.8 16.8 %all_to_all.10.got_ref = bf16[32,16,128]{2,1,0:T(8,128)(2,1)} all-to-all(bf16[32,16,128]{2,1,0:T(8,128)(2,1)S(1)} %add_convert_fusion), channel_id=1, replica_groups=mesh['zl'=4,'y'=4,'core'=2,'zh'=2,'x'=4] {'y','zh','zl'}, dimensions={0} | all-to-all | bytes 262144 | tf_op jit(solution)/shard_map/all_to_all | solution.py:329
  73.5 1.6 %shard_map.103 = bf16[32,16,128]{2,1,0:T(8,128)(2,1)} custom-call(bf16[32,16,128]{2,1,0:T(8,128)(2,1)} %all_to_all.10.got_ref), custom_call_target="tpu_custom_call" | custom-call | bytes 131072 | tf_op jit(solution)/shard_map/pallas_call | solution.py:246
  75.1 14.3 %all_to_all.11.own_ref = bf16[32,16,128]{2,1,0:T(8,128)(2,1)S(1)} all-to-all(bf16[32,16,128]{2,1,0:T(8,128)(2,1)} %shard_map.103), channel_id=1, replica_groups=mesh['zl'=4,'y'=4,'core'=2,'zh'=2,'x'=4] {'y','zh','zl'}, dimensions={0} | all-to-all | bytes 262144 | tf_op jit(solution)/shard_map/all_to_all | solution.py:331
  89.4 1.3 %collective-permute-done.8.other_ref = bf16[32,16,128]{2,1,0:T(8,128)(2,1)S(1)} collective-permute-done((bf16[32,16,128]{2,1,0:T(8,128)(2,1)S(1)}, bf16[32,16,128]{2,1,0:T(8,128)(2,1)S(1)}, u32[]{:S(2)}, u32[]{:S(2)}) %collective-permute-start.8) | collective-permute-done | bytes 131104 | tf_op jit(solution)/shard_map/ppermute | solution.py:332
  91.4 1.9 %shard_map.104 = (f32[128,512]{1,0:T(8,128)}, f32[128,512]{1,0:T(8,128)}) custom-call(s32[1]{0:T(128)} %bitcast.5.core_ref, bf16[32,16,128]{2,1,0:T(8,128)(2,1)} %copy-done.1, bf16[32,16,128]{2,1,0:T(8,128)(2,1)} %copy-done.9, f32[128,512]{1,0:T(8,128)} %amp_ref.3), custom_call_target="tpu_custom_call" | custom-call | bytes 524288 | tf_op jit(solution)/shard_map/pallas_call | solution.py:246
  (35 shorter events, 4.1 us)
Async XLA Ops:
  0.6 18.9 %copy-start = (f32[1,256,1024]{2,1,0:T(8,128)S(1)}, f32[1,256,1024]{2,1,0:T(8,128)}, u32[]{:S(2)}) copy-start(f32[1,256,1024]{2,1,0:T(8,128)} %param.12) | copy-start | bytes 3145732
  0.6 7.2 %copy-start.10 = (s32[1,2]{1,0:T(1,128)S(1)}, s32[1,2]{1,0:T(1,128)}, u32[]{:S(2)}) copy-start(s32[1,2]{1,0:T(1,128)} %offset_ref.1) | copy-start | bytes 28
  0.7 19.8 %copy-start.5 = (s32[256,1024]{1,0:T(8,128)S(1)}, s32[256,1024]{1,0:T(8,128)}, u32[]{:S(2)}) copy-start(s32[256,1024]{1,0:T(8,128)} %param.13) | copy-start | bytes 3145732
  3.1 22.5 %collective-permute-start.3 = (bf16[128,1024]{1,0:T(8,128)(2,1)}, bf16[128,1024]{1,0:T(8,128)(2,1)S(1)}, u32[]{:S(2)}, u32[]{:S(2)}) collective-permute-start(bf16[128,1024]{1,0:T(8,128)(2,1)} %shard_map.96.e0.pupil_ref), channel_id=1, source_target_pairs={{0,1},{1,2},{2,3},{3,0},{4,5},{5,6},{6,7},{7,4},{8,9},{9,10},{10,1... | collective-permute-start | bytes 786440 | tf_op jit(solution)/shard_map/ppermute | solution.py:312
  4.6 21.0 %collective-permute-start.2 = (bf16[128,1024]{1,0:T(8,128)(2,1)}, bf16[128,1024]{1,0:T(8,128)(2,1)S(1)}, u32[]{:S(2)}, u32[]{:S(2)}) collective-permute-start(bf16[128,1024]{1,0:T(8,128)(2,1)} %shard_map.96.e0.pupil_ref), channel_id=1, source_target_pairs={{0,2},{1,3},{2,0},{3,1},{4,6},{5,7},{6,4},{7,5},{8,10},{9,11},{10,... | collective-permute-start | bytes 786440 | tf_op jit(solution)/shard_map/ppermute | solution.py:312
  7.4 18.2 %collective-permute-start.1 = (bf16[128,1024]{1,0:T(8,128)(2,1)}, bf16[128,1024]{1,0:T(8,128)(2,1)S(1)}, u32[]{:S(2)}, u32[]{:S(2)}) collective-permute-start(bf16[128,1024]{1,0:T(8,128)(2,1)} %shard_map.96.e0.pupil_ref), channel_id=1, source_target_pairs={{0,3},{1,0},{2,1},{3,2},{4,7},{5,4},{6,5},{7,6},{8,11},{9,8},{10,9... | collective-permute-start | bytes 786440 | tf_op jit(solution)/shard_map/ppermute | solution.py:312
  7.9 13.4 %collective-permute-start = (s32[1,2]{1,0:T(1,128)S(1)}, s32[1,2]{1,0:T(1,128)S(1)}, u32[]{:S(2)}, u32[]{:S(2)}) collective-permute-start(s32[1,2]{1,0:T(1,128)S(1)} %copy-done.10), channel_id=1, source_target_pairs={{0,4},{4,0},{1,5},{5,1},{2,6},{6,2},{3,7},{7,3},{8,12},{12,8},{9,1... | collective-permute-start | bytes 32 | tf_op jit(solution)/shard_map/ppermute | solution.py:313
  21.3 0.5 copy-start.11
  25.6 0.7 copy-start.2
  25.6 0.8 copy-start.4
  25.6 0.8 copy-start.3
  36.5 11.2 %collective-permute-start.4 = (bf16[128,1024]{1,0:T(8,128)(2,1)}, bf16[128,1024]{1,0:T(8,128)(2,1)S(1)}, u32[]{:S(2)}, u32[]{:S(2)}) collective-permute-start(bf16[128,1024]{1,0:T(8,128)(2,1)} %shard_map.99), channel_id=1, source_target_pairs={{0,2},{1,3},{2,0},{3,1},{4,6},{5,7},{6,4},{7,5},{8,10},{9,11},{10,... | collective-permute-start | bytes 786440 | tf_op jit(solution)/shard_map/ppermute | solution.py:322
  39.6 9.6 %collective-permute-start.5 = (bf16[128,1024]{1,0:T(8,128)(2,1)}, bf16[128,1024]{1,0:T(8,128)(2,1)S(1)}, u32[]{:S(2)}, u32[]{:S(2)}) collective-permute-start(bf16[128,1024]{1,0:T(8,128)(2,1)} %shard_map.100), channel_id=1, source_target_pairs={{0,1},{1,2},{2,3},{3,0},{4,5},{5,6},{6,7},{7,4},{8,9},{9,10},{10,1... | collective-permute-start | bytes 786440 | tf_op jit(solution)/shard_map/ppermute | solution.py:322
  44.9 6.6 %collective-permute-start.6 = (bf16[128,1024]{1,0:T(8,128)(2,1)}, bf16[128,1024]{1,0:T(8,128)(2,1)S(1)}, u32[]{:S(2)}, u32[]{:S(2)}) collective-permute-start(bf16[128,1024]{1,0:T(8,128)(2,1)} %shard_map.101), channel_id=1, source_target_pairs={{0,3},{1,0},{2,1},{3,2},{4,7},{5,4},{6,5},{7,6},{8,11},{9,8},{10,9... | collective-permute-start | bytes 786440 | tf_op jit(solution)/shard_map/ppermute | solution.py:322
  47.7 3.8 %copy-start.6 = (bf16[128,1024]{1,0:T(8,128)(2,1)}, bf16[128,1024]{1,0:T(8,128)(2,1)S(1)}, u32[]{:S(2)}) copy-start(bf16[128,1024]{1,0:T(8,128)(2,1)S(1)} %collective-permute-done.4.s1) | copy-start | bytes 786436
  49.2 2.4 %copy-start.7 = (bf16[128,1024]{1,0:T(8,128)(2,1)}, bf16[128,1024]{1,0:T(8,128)(2,1)S(1)}, u32[]{:S(2)}) copy-start(bf16[128,1024]{1,0:T(8,128)(2,1)S(1)} %collective-permute-done.5.s2) | copy-start | bytes 786436
  51.5 0.7 copy-start.8
  54.3 1.6 %collective-permute-start.7 = (bf16[32,16,128]{2,1,0:T(8,128)(2,1)}, bf16[32,16,128]{2,1,0:T(8,128)(2,1)S(1)}, u32[]{:S(2)}, u32[]{:S(2)}) collective-permute-start(bf16[32,16,128]{2,1,0:T(8,128)(2,1)} %get-tuple-element.24), channel_id=1, source_target_pairs={{0,8},{8,0},{1,9},{9,1},{2,10},{10,2},{3,11},{11,3},{4,12},{12,4},... | collective-permute-start | bytes 393224 | tf_op jit(solution)/shard_map/ppermute | solution.py:327
  89.4 1.4 %copy-start.1 = (bf16[32,16,128]{2,1,0:T(8,128)(2,1)}, bf16[32,16,128]{2,1,0:T(8,128)(2,1)S(1)}, u32[]{:S(2)}) copy-start(bf16[32,16,128]{2,1,0:T(8,128)(2,1)S(1)} %all_to_all.11.own_ref) | copy-start | bytes 393220
  89.4 1.3 %collective-permute-start.8 = (bf16[32,16,128]{2,1,0:T(8,128)(2,1)S(1)}, bf16[32,16,128]{2,1,0:T(8,128)(2,1)S(1)}, u32[]{:S(2)}, u32[]{:S(2)}) collective-permute-start(bf16[32,16,128]{2,1,0:T(8,128)(2,1)S(1)} %all_to_all.11.own_ref), channel_id=1, source_target_pairs={{0,8},{8,0},{1,9},{9,1},{2,10},{10,2},{3,11},{11,3},{4,12},{12,4},... | collective-permute-start | bytes 393224 | tf_op jit(solution)/shard_map/ppermute | solution.py:332
  90.8 0.7 copy-start.9
